TPU v7x, 32 devices: a whole 2x2x4 slice. The times are simulated.
32 devices in a mesh: abl: 2 (over y), head: 4 (over x, core), ctx: 4 (over z).
Axes of the slice: x: 2, y: 2, z: 4, core: 2. Of those that a mesh axis runs over, the one named last changes fastest.
Arguments:
- queries: bfloat16 [1024, 6144], P(('abl', 'head', 'ctx')), parts along dimension 0, may hold values from -30 to 30
- keys: bfloat16 [16384, 6144], P(('abl', 'ctx'), 'head'), parts along dimension 0, may hold values from -6 to 6
- values: bfloat16 [16384, 6144], P(('abl', 'ctx'), 'head'), parts along dimension 0, may hold values from -6 to 6
- kept_rows: int32 [128], P(('abl', 'ctx')), parts along dimension 0, may hold values from 0 to 1, as said below
- out_weight: bfloat16 [6144, 6144], P('head'), may hold values from -6 to 6
Outputs:
- projected: bfloat16 [1024, 6144], P(('abl', 'head', 'ctx')), parts along dimension 0
There are 2 independent parts, one for each index of `abl`. A program takes and returns all parts, laid end to end along the dimension named above; an argument that names none is the same for every part. Nothing has to cross between parts.
Inputs may be any that keep to these rules, and one draw needn't show every extreme that they name: `kept_rows`: in every part the first row of each block of 16 consecutive rows is kept.
All inputs are finite; a program needn't handle non-finite values.
Results may differ from a plain program's by a relative error of at most 0.028.
Values may be sent and summed in bfloat16 or wider, within the bound.
No kernel may reach another device: no remote copies, remote signals or barrier semaphores. Data moves between devices by JAX's collectives and lax.ppermute only.
A program may use at most 128 MiB of HBM per device.

v0:
```python
import math
import jax
import jax.numpy as jnp
from jax import lax
from jax.sharding import PartitionSpec as P

HD = 128


def shards(queries, keys, values, kept_rows, out_weight):
    score_scale = 1.0 / math.sqrt(HD)
    local_heads = keys.shape[1] // HD
    key_count = keys.shape[0]
    key_heads = keys.reshape(key_count, local_heads, HD)
    value_heads = values.reshape(key_count, local_heads, HD)
    visible = jnp.repeat(kept_rows, 128) > 0
    query_block = lax.all_to_all(queries, "head", split_axis=1, concat_axis=0, tiled=True)
    all_queries = lax.all_gather(query_block, "ctx", axis=0, tiled=True)
    row_count = all_queries.shape[0]
    zeros_sum = jnp.zeros((row_count, local_heads * HD), jnp.float32)
    lowest = jnp.full((local_heads, row_count), -1e30, jnp.float32)
    summed = zeros_sum
    row_count = all_queries.shape[0]
    shaped = all_queries.reshape(row_count, local_heads, HD)
    scores = (
        jnp.einsum("qhd,khd->hqk", shaped, key_heads, preferred_element_type=jnp.float32)
        * score_scale
    )
    scores = jnp.where(visible[None, None, :], scores, -jnp.inf)
    highest = jnp.maximum(lowest, jnp.max(scores, axis=-1))
    rescale = jnp.exp(lowest - highest)
    softened = jnp.exp(scores - highest[..., None])
    normal_sum = jnp.sum(softened, axis=-1)
    mixed = jnp.einsum(
        "hqk,khd->qhd",
        softened.astype(jnp.bfloat16),
        value_heads,
        preferred_element_type=jnp.float32,
    )
    summed = summed * jnp.repeat(rescale.T, HD, axis=1) + mixed.reshape(row_count, local_heads * HD)
    summed, running, normal_sum = (summed, highest, normal_sum)
    highest = lax.pmax(running, "ctx")
    rescale = jnp.exp(running - highest)
    summed = summed * jnp.repeat(rescale.T, HD, axis=1)
    normal_sum = normal_sum * rescale
    summed, normal_sum = (
        lax.psum_scatter(
            summed.astype(jnp.bfloat16), "ctx", scatter_dimension=0, tiled=True
        ).astype(jnp.float32),
        lax.psum_scatter(
            normal_sum.astype(jnp.bfloat16), "ctx", scatter_dimension=1, tiled=True
        ).astype(jnp.float32),
    )
    attended = (summed / jnp.repeat(normal_sum.T, HD, axis=1)).astype(jnp.bfloat16)
    return lax.psum_scatter(
        jnp.dot(attended, out_weight, preferred_element_type=jnp.float32).astype(jnp.bfloat16),
        "head",
        scatter_dimension=0,
        tiled=True,
    )


def solution(mesh):
    placed = (
        P(("abl", "head", "ctx"), None),
        P(("abl", "ctx"), "head"),
        P(("abl", "ctx"), "head"),
        P(("abl", "ctx")),
        P("head", None),
    )
    return jax.shard_map(
        shards,
        mesh=mesh,
        in_specs=placed,
        out_specs=P(("abl", "head", "ctx"), None),
        check_vma=False,
    )
```

profile of v0, /device:TPU:0, one launch (start us, length us, event | category | flops | bytes accessed | tf_op | source)
XLA Modules:
  0.0 223.1 jit_solution(14071060724346164999)
XLA Ops:
  6.5 1.0 copy.33
  7.6 11.6 %all_to_all.19 = bf16[32,4,1536]{2,0,1:T(8,128)(2,1)} all-to-all(bf16[32,4,1536]{2,0,1:T(8,128)(2,1)S(1)} %bitcast.42), channel_id=1, replica_groups=mesh['abl'=2,'head'=4,'ctx'=4] {'head'}, dimensions={1} | all-to-all | bytes 786432 | tf_op jit(solution)/shard_map/all_to_all | solution.py:17
  19.1 0.0 all-gather.2.cloned.1.call-update
  19.2 0.0 reduce-scatter.12.cloned.1.call-start
  19.2 8.8 %copy.21 = bf16[2048,1536]{0,1:T(8,128)(2,1)} copy(bf16[2048,1536]{1,0:T(8,128)(2,1)} %param.6) | data formatting | bytes 12582912 | tf_op args[1]
  28.0 8.8 %copy.24 = bf16[2048,1536]{0,1:T(8,128)(2,1)} copy(bf16[2048,1536]{1,0:T(8,128)(2,1)} %param.7) | data formatting | bytes 12582912 | tf_op args[2]
  36.7 0.1 broadcast_bitcast_fusion
  36.8 20.3 %all-gather.2.cloned.1.call-done = bf16[512,1536]{1,0:T(8,128)(2,1)} async-done(((bf16[128,1536]{1,0:T(8,128)(2,1)}), bf16[512,1536]{1,0:T(8,128)(2,1)}) %all-gather.2.cloned.1.call-update) | async-done | bytes 1572880 | tf_op jit(solution)/shard_map/all_gather | solution.py:18
  57.1 1.7 copy.20
  58.8 22.6 %fusion = (f32[12,512]{1,0:T(8,128)S(1)}, f32[12,512,2048]{2,1,0:T(8,128)}) fusion(pred[2048]{0:T(1024)(128)(4,1)S(1)} %broadcast_bitcast_fusion, bf16[512,12,128]{0,2,1:T(8,128)(2,1)S(1)} %bitcast.38, bf16[2048,12,128]{0,2,1:T(8,128)(2,1)} %bitcast.37), kind=kOutput, calls=%fused_computation.2 | convolution fusion | flops 3258968064 | bytes 58222592 | tf_op jit(solution)/shard_map/qhd,khd->hqk/dot_general | solution.py:26
  81.4 16.9 %pmax.7 = f32[12,512]{1,0:T(8,128)S(1)} all-reduce(f32[12,512]{1,0:T(8,128)S(1)} %broadcast_maximum_fusion), channel_id=1, replica_groups=mesh['abl'=2,'head'=4,'ctx'=4] {'ctx'}, use_global_device_ids=true, to_apply=%region_1.2 | all-reduce | flops 6144 | bytes 49152 | tf_op jit(solution)/shard_map/pmax | solution.py:42
  98.4 21.1 %fusion.1 = f32[12,512]{1,0:T(8,128)S(1)} fusion(f32[12,512,2048]{2,1,0:T(8,128)} %get-tuple-element.9, f32[12,512]{1,0:T(8,128)S(1)} %broadcast_maximum_fusion, pred[2048]{0:T(1024)(128)(4,1)S(1)} %broadcast_bitcast_fusion), kind=kLoop, calls=%fused_computation.3 | loop fusion | flops 50325504 | bytes 50382848 | tf_op jit(solution)/shard_map/reduce_sum | solution.py:33
  119.5 0.8 copy.29
  120.3 0.0 reduce-scatter.10.cloned.1.call-start
  120.4 22.0 %fusion.7 = bf16[512,12,128]{0,2,1:T(8,128)(2,1)S(1)} fusion(bf16[2048,12,128]{0,2,1:T(8,128)(2,1)} %bitcast.39, f32[12,512,2048]{2,1,0:T(8,128)} %get-tuple-element.9, f32[12,512]{1,0:T(8,128)S(1)} %broadcast_maximum_fusion, pred[2048]{0:T(1024)(128)(4,1)S(1)} %broadcast_bitcast_fusion, f32[512,12]{0,1:T(8,128)S(1)} %get-tuple-element.6, ...), kind=kOutput, calls=%fused_computation.10 | convolution fusion | flops 3273916416 | bytes 58271744 | tf_op jit(solution)/shard_map/hqk,khd->qhd/dot_general | solution.py:34
  142.4 1.6 copy.27
  144.0 0.2 reduce-scatter.8.cloned.1.call-start
  144.2 0.0 reduce-scatter.12.cloned.1.call-done
  144.3 0.8 copy.30
  145.1 32.7 %reduce-scatter.10.cloned.1.call-done = bf16[128,1536]{1,0:T(8,128)(2,1)} async-done(((bf16[512,1536]{1,0:T(8,128)(2,1)}), bf16[128,1536]{1,0:T(8,128)(2,1)}) %reduce-scatter.10.cloned.1.call-update) | async-done | bytes 393232
  177.7 1.2 copy.28
  179.0 0.1 fusion.10
  179.1 10.2 %convolution_convert_fusion = bf16[128,6144]{1,0:T(8,128)(2,1)} fusion(bf16[128,1536]{0,1:T(8,128)(2,1)S(1)} %fusion.10, bf16[1536,6144]{1,0:T(8,128)(2,1)} %param.9), kind=kOutput, calls=%fused_computation.7 | convolution fusion | flops 2416705536 | bytes 20840448 | tf_op jit(solution)/shard_map/dot_general | solution.py:56
  189.3 27.3 %reduce-scatter.8.cloned.1.call-done = bf16[32,6144]{1,0:T(8,128)(2,1)} async-done(((bf16[128,6144]{1,0:T(8,128)(2,1)}), bf16[32,6144]{1,0:T(8,128)(2,1)}) %reduce-scatter.8.cloned.1.call-update) | async-done | bytes 393232 | tf_op jit(solution)/shard_map/reduce_scatter | solution.py:55
  (10 shorter events, 0.1 us)
Async XLA Ops:
  6.5 30.2 %copy-start = (s32[16]{0:T(128)S(1)}, s32[16]{0:T(128)}, u32[]{:S(2)}) copy-start(s32[16]{0:T(128)} %param.8) | copy-start | bytes 196
  6.5 50.6 %all-gather.2.cloned.1.call-start = ((), (), s32[]{:S(2)}) async-start(), calls=%async_computation.4 | async-start | bytes 1966080 | tf_op jit(solution)/shard_map/all_gather | solution.py:18
  19.2 125.1 %reduce-scatter.12.cloned.1.call-start = ((), (), s32[]{:S(2)}) async-start(), calls=%async_computation.7 | async-start | bytes 163840
  120.3 57.4 %reduce-scatter.10.cloned.1.call-start = ((), (), s32[]{:S(2)}) async-start(), calls=%async_computation.6 | async-start | bytes 1966080
  144.0 72.6 %reduce-scatter.8.cloned.1.call-start = ((), (), s32[]{:S(2)}) async-start(), calls=%async_computation.5 | async-start | bytes 1966080 | tf_op jit(solution)/shard_map/reduce_scatter | solution.py:55
Sparse Core Ops, SparseCore 0:
  19.3 37.8 all-gather.1
  120.4 17.4 reduce-scatter.11
  144.1 33.5 reduce-scatter.9
  189.4 27.1 reduce-scatter.7
where the time goes:
time: 224 us; the launch traced here: 223 us
  waiting for transfers between devices  80.4 us (36%)
  matrix products  54.9 us (25%)
  blocking collectives  28.5 us (13%)
  local copies, waits for them, and re-layouts  24.7 us (11%)
  other arithmetic  21.2 us (9%)
  between operations  13.2 us (6%)
    unnamed x6, waiting for transfers between devices  32.7 us
    reduce_scatter x1, waiting for transfers between devices, shards(): lax.psum_scatter(jnp.dot(attended, out_weight, preferred_element_type=jnp...  27.3 us
    dot_general x1, matrix products, shards(): jnp.einsum('qhd,khd->hqk', shaped, key_heads, preferred_element_type=jnp....  22.6 us
    dot_general x1, matrix products, shards(): jnp.einsum('hqk,khd->qhd', softened.astype(jnp.bfloat16), value_heads, pr...  22 us
    unnamed x8, local copies, waits for them, and re-layouts  21.9 us
    reduce_sum x1, other arithmetic, shards(): normal_sum = jnp.sum(softened, axis=-1)  21.1 us
    all_gather x1, waiting for transfers between devices, shards(): all_queries = lax.all_gather(query_block, 'ctx', axis=0, tiled=True)  20.3 us
    pmax x1, blocking collectives, shards(): highest = lax.pmax(running, 'ctx')  16.9 us
  transfers between devices with their start and end apart: 4, of which 3 were waited for; matrix products, arithmetic and copies ran while one was open for 19% of the time, Pallas kernels for 0%

commit v1 on v0

--- a/solution.py
+++ b/solution.py
@@ -5,6 +5,28 @@
 from jax.sharding import PartitionSpec as P
 
 HD = 128
+
+
+def in_order(blocks, dim):
+    dims = list(blocks.shape[1:])
+    dims[dim] *= blocks.shape[0]
+    return jnp.moveaxis(blocks, 0, dim).reshape(dims)
+
+
+def ring_gather(x, axis, dim):
+    size = lax.axis_size(axis)
+    pairs = [(i, (i + 1) % size) for i in range(size)]
+    back = [(b, a) for a, b in pairs]
+    lower, upper = ([], [])
+    for turn in range(size - 1):
+        if turn % 2 == 0:
+            lower.append(lax.ppermute(lower[-1] if lower else x, axis, pairs))
+        else:
+            upper.append(lax.ppermute(upper[-1] if upper else x, axis, back))
+    blocks = jnp.stack([*lower[::-1], x, *upper])
+    shift = lax.axis_index(axis) - len(lower)
+    blocks = blocks[(jnp.arange(size) - shift) % size]
+    return in_order(blocks, dim)
 
 
 def shards(queries, keys, values, kept_rows, out_weight):
@@ -15,7 +37,7 @@
     value_heads = values.reshape(key_count, local_heads, HD)
     visible = jnp.repeat(kept_rows, 128) > 0
     query_block = lax.all_to_all(queries, "head", split_axis=1, concat_axis=0, tiled=True)
-    all_queries = lax.all_gather(query_block, "ctx", axis=0, tiled=True)
+    all_queries = ring_gather(query_block, "ctx", 0)
     row_count = all_queries.shape[0]
     zeros_sum = jnp.zeros((row_count, local_heads * HD), jnp.float32)
     lowest = jnp.full((local_heads, row_count), -1e30, jnp.float32)

time: 224 us -> 229 us (1.022)
  starting transfers between devices: 0.31 us -> 4.15 us
  local copies, waits for them, and re-layouts: 24.7 us -> 27.6 us
  waiting for transfers between devices: 80.4 us -> 77.6 us
    all_gather x1 -> x0, waiting for transfers between devices: 20.3 us -> none  [shards(): all_queries = lax.all_gather(query_block, 'ctx', axis=0, tiled=True)]
    ppermute x0 -> x3, waiting for transfers between devices: none -> 18.3 us  [the longest x1 9.47 us: ring_gather(): upper.append(lax.ppermute(upper[-1] if upper else x, axis, back))]
    ppermute x0 -> x3, starting transfers between devices: none -> 3.88 us  [the longest x1 2.3 us: ring_gather(): upper.append(lax.ppermute(upper[-1] if upper else x, axis, back))]
    another operation x0 -> x1, local copies, waits for them, and re-layouts: none -> 2.89 us  [shards(): shaped = all_queries.reshape(row_count, local_heads, HD)]
    unnamed x6 -> x5, waiting for transfers between devices: 32.7 us -> 32 us
  transfers between devices with their start and end apart: 4 -> 6, of which waited for: 3 -> 4; matrix products, arithmetic and copies ran while one was open for 19% -> 18% of each run, Pallas kernels for 0% -> 0%
where the time goes in v1:
time: 229 us; the launch traced here: 228 us
  waiting for transfers between devices  77.6 us (34%)
  matrix products  55.2 us (24%)
  blocking collectives  28.9 us (13%)
  local copies, waits for them, and re-layouts  27.6 us (12%)
  other arithmetic  21.4 us (9%)
  between operations  13.2 us (6%)
  starting transfers between devices  4.15 us (2%)
    unnamed x5, waiting for transfers between devices  32 us
    reduce_scatter x1, waiting for transfers between devices, shards(): lax.psum_scatter(jnp.dot(attended, out_weight, preferred_element_type=jnp...  27.3 us
    dot_general x1, matrix products, shards(): jnp.einsum('qhd,khd->hqk', shaped, key_heads, preferred_element_type=jnp....  22.9 us
    dot_general x1, matrix products, shards(): jnp.einsum('hqk,khd->qhd', softened.astype(jnp.bfloat16), value_heads, pr...  22 us
    unnamed x8, local copies, waits for them, and re-layouts  21.8 us
    reduce_sum x1, other arithmetic, shards(): normal_sum = jnp.sum(softened, axis=-1)  21.1 us
    pmax x1, blocking collectives, shards(): highest = lax.pmax(running, 'ctx')  17.4 us
    all_to_all x1, blocking collectives, shards(): lax.all_to_all(queries, 'head', split_axis=1, concat_axis=0, tiled=True)  11.5 us
  transfers between devices with their start and end apart: 6, of which 4 were waited for; matrix products, arithmetic and copies ran while one was open for 18% of the time, Pallas kernels for 0%

profile of v1, /device:TPU:0, one launch (start us, length us, event | category | flops | bytes accessed | tf_op | source)
XLA Modules:
  0.0 228.0 jit_solution(7476263701949374718)
XLA Ops:
  6.5 1.0 copy.41
  7.6 11.5 %all_to_all.19 = bf16[32,4,1536]{2,0,1:T(8,128)(2,1)S(1)} all-to-all(bf16[32,4,1536]{2,0,1:T(8,128)(2,1)S(1)} %bitcast.48), channel_id=1, replica_groups=mesh['abl'=2,'head'=4,'ctx'=4] {'head'}, dimensions={1} | all-to-all | bytes 786432 | tf_op jit(solution)/shard_map/all_to_all | solution.py:39
  19.0 1.6 collective-permute-start
  20.6 8.7 %copy.22 = bf16[2048,1536]{0,1:T(8,128)(2,1)} copy(bf16[2048,1536]{1,0:T(8,128)(2,1)} %param.6) | data formatting | bytes 12582912 | tf_op args[1]
  29.3 8.7 %copy.25 = bf16[2048,1536]{0,1:T(8,128)(2,1)} copy(bf16[2048,1536]{1,0:T(8,128)(2,1)} %param.7) | data formatting | bytes 12582912 | tf_op args[2]
  38.0 2.3 %collective-permute-start.2 = (bf16[128,1536]{1,0:T(8,128)(2,1)S(1)}, bf16[128,1536]{1,0:T(8,128)(2,1)S(1)}, u32[]{:S(2)}, u32[]{:S(2)}) collective-permute-start(bf16[128,1536]{1,0:T(8,128)(2,1)S(1)} %bitcast.46), channel_id=1, source_target_pairs={{1,0},{2,1},{3,2},{0,3},{5,4},{6,5},{7,6},{4,7},{9,8},{10,9},{11,1... | collective-permute-start | bytes 1179656 | tf_op jit(solution)/shard_map/ppermute | solution.py:25
  40.4 9.5 %collective-permute-done.2 = bf16[128,1536]{1,0:T(8,128)(2,1)S(1)} collective-permute-done((bf16[128,1536]{1,0:T(8,128)(2,1)S(1)}, bf16[128,1536]{1,0:T(8,128)(2,1)S(1)}, u32[]{:S(2)}, u32[]{:S(2)}) %collective-permute-start.2) | collective-permute-done | bytes 393248 | tf_op jit(solution)/shard_map/ppermute | solution.py:25
  49.9 8.8 %collective-permute-done.1 = bf16[128,1536]{1,0:T(8,128)(2,1)S(1)} collective-permute-done((bf16[128,1536]{1,0:T(8,128)(2,1)S(1)}, bf16[128,1536]{1,0:T(8,128)(2,1)S(1)}, u32[]{:S(2)}, u32[]{:S(2)}) %collective-permute-start.1) | collective-permute-done | bytes 393248 | tf_op jit(solution)/shard_map/ppermute | solution.py:23
  58.7 0.2 pad_maximum_fusion
  58.9 1.8 gather_fusion
  60.7 2.9 %reshape.94 = bf16[512,12,128]{2,1,0:T(8,128)(2,1)S(1)} reshape(bf16[4,128,1536]{2,1,0:T(8,128)(2,1)} %gather_fusion) | data formatting | bytes 3145728 | tf_op jit(solution)/shard_map/reshape;reshape | solution.py:46
  63.6 22.9 %fusion = (f32[12,512]{1,0:T(8,128)S(1)}, f32[12,512,2048]{2,1,0:T(8,128)}) fusion(pred[2048]{0:T(1024)(128)(4,1)S(1)} %broadcast_bitcast_fusion, bf16[2048,12,128]{0,2,1:T(8,128)(2,1)} %bitcast.42, bf16[512,12,128]{2,1,0:T(8,128)(2,1)S(1)} %reshape.94), kind=kOutput, calls=%fused_computation.3 | convolution fusion | flops 3258968064 | bytes 58222592 | tf_op jit(solution)/shard_map/qhd,khd->hqk/dot_general | solution.py:48
  86.6 17.4 %pmax.7 = f32[12,512]{1,0:T(8,128)S(1)} all-reduce(f32[12,512]{1,0:T(8,128)S(1)} %broadcast_maximum_fusion), channel_id=1, replica_groups=mesh['abl'=2,'head'=4,'ctx'=4] {'ctx'}, use_global_device_ids=true, to_apply=%region_1.2 | all-reduce | flops 6144 | bytes 49152 | tf_op jit(solution)/shard_map/pmax | solution.py:64
  104.0 21.1 %fusion.1 = f32[12,512]{1,0:T(8,128)S(1)} fusion(f32[12,512,2048]{2,1,0:T(8,128)} %get-tuple-element.9, f32[12,512]{1,0:T(8,128)S(1)} %broadcast_maximum_fusion, pred[2048]{0:T(1024)(128)(4,1)S(1)} %broadcast_bitcast_fusion), kind=kLoop, calls=%fused_computation.4 | loop fusion | flops 50325504 | bytes 50382848 | tf_op jit(solution)/shard_map/reduce_sum | solution.py:55
  125.1 0.8 copy.33
  126.0 22.0 %fusion.7 = bf16[512,12,128]{0,2,1:T(8,128)(2,1)S(1)} fusion(bf16[2048,12,128]{0,2,1:T(8,128)(2,1)} %bitcast.43, f32[12,512,2048]{2,1,0:T(8,128)} %get-tuple-element.9, f32[12,512]{1,0:T(8,128)S(1)} %broadcast_maximum_fusion, pred[2048]{0:T(1024)(128)(4,1)S(1)} %broadcast_bitcast_fusion, f32[512,12]{0,1:T(8,128)S(1)} %get-tuple-element.6, ...), kind=kOutput, calls=%fused_computation.11 | convolution fusion | flops 3273916416 | bytes 58271744 | tf_op jit(solution)/shard_map/hqk,khd->qhd/dot_general | solution.py:56
  148.0 1.6 copy.31
  149.6 0.2 reduce-scatter.8.cloned.1.call-start
  149.9 0.8 copy.34
  150.7 31.9 %reduce-scatter.10.cloned.1.call-done = bf16[128,1536]{1,0:T(8,128)(2,1)} async-done(((bf16[512,1536]{1,0:T(8,128)(2,1)}), bf16[128,1536]{1,0:T(8,128)(2,1)}) %reduce-scatter.10.cloned.1.call-update) | async-done | bytes 393232
  182.6 1.2 copy.32
  183.8 0.1 fusion.12
  183.9 10.2 %convolution_convert_fusion = bf16[128,6144]{1,0:T(8,128)(2,1)} fusion(bf16[128,1536]{0,1:T(8,128)(2,1)S(1)} %fusion.12, bf16[1536,6144]{1,0:T(8,128)(2,1)} %param.9), kind=kOutput, calls=%fused_computation.8 | convolution fusion | flops 2416705536 | bytes 20840448 | tf_op jit(solution)/shard_map/dot_general | solution.py:78
  194.2 27.3 %reduce-scatter.8.cloned.1.call-done = bf16[32,6144]{1,0:T(8,128)(2,1)} async-done(((bf16[128,6144]{1,0:T(8,128)(2,1)}), bf16[32,6144]{1,0:T(8,128)(2,1)}) %reduce-scatter.8.cloned.1.call-update) | async-done | bytes 393232 | tf_op jit(solution)/shard_map/reduce_scatter | solution.py:77
  (17 shorter events, 0.3 us)
Async XLA Ops:
  6.5 143.4 %reduce-scatter.12.cloned.1.call-start = ((), (), s32[]{:S(2)}) async-start(), calls=%async_computation.6 | async-start | bytes 163840
  19.0 21.3 %collective-permute-start = (bf16[128,1536]{1,0:T(8,128)(2,1)S(1)}, bf16[128,1536]{1,0:T(8,128)(2,1)S(1)}, u32[]{:S(2)}, u32[]{:S(2)}) collective-permute-start(bf16[128,1536]{1,0:T(8,128)(2,1)S(1)} %bitcast.45), channel_id=1, source_target_pairs={{0,1},{1,2},{2,3},{3,0},{4,5},{5,6},{6,7},{7,4},{8,9},{9,10},{10,1... | collective-permute-start | bytes 1179656 | tf_op jit(solution)/shard_map/ppermute | solution.py:23
  29.3 11.0 %copy-start = (s32[16]{0:T(128)S(1)}, s32[16]{0:T(128)}, u32[]{:S(2)}) copy-start(s32[16]{0:T(128)} %param.8) | copy-start | bytes 196
  38.0 11.9 %collective-permute-start.2 = (bf16[128,1536]{1,0:T(8,128)(2,1)S(1)}, bf16[128,1536]{1,0:T(8,128)(2,1)S(1)}, u32[]{:S(2)}, u32[]{:S(2)}) collective-permute-start(bf16[128,1536]{1,0:T(8,128)(2,1)S(1)} %bitcast.46), channel_id=1, source_target_pairs={{1,0},{2,1},{3,2},{0,3},{5,4},{6,5},{7,6},{4,7},{9,8},{10,9},{11,1... | collective-permute-start | bytes 1179656 | tf_op jit(solution)/shard_map/ppermute | solution.py:25
  40.3 18.4 %collective-permute-start.1 = (bf16[128,1536]{1,0:T(8,128)(2,1)S(1)}, bf16[128,1536]{1,0:T(8,128)(2,1)S(1)}, u32[]{:S(2)}, u32[]{:S(2)}) collective-permute-start(bf16[128,1536]{1,0:T(8,128)(2,1)S(1)} %collective-permute-done), channel_id=1, source_target_pairs={{0,1},{1,2},{2,3},{3,0},{4,5},{5,6},{6,7},{7,4},{8,9},{9,10},{10,1... | collective-permute-start | bytes 1179656 | tf_op jit(solution)/shard_map/ppermute | solution.py:23
  125.9 56.7 %reduce-scatter.10.cloned.1.call-start = ((), (), s32[]{:S(2)}) async-start(), calls=%async_computation.5 | async-start | bytes 1966080
  149.6 71.9 %reduce-scatter.8.cloned.1.call-start = ((), (), s32[]{:S(2)}) async-start(), calls=%async_computation.4 | async-start | bytes 1966080 | tf_op jit(solution)/shard_map/reduce_scatter | solution.py:77
Sparse Core Ops, SparseCore 0:
  126.1 16.7 reduce-scatter.11
  149.8 32.8 reduce-scatter.9
  194.3 27.1 reduce-scatter.7
